TPU v7x, 256 devices: a whole 4x4x8 slice. The times are simulated.
256 devices in a mesh: rows: 64 (over y, z, core), feat: 4 (over x).
Axes of the slice: x: 4, y: 4, z: 8, core: 2. Of those that a mesh axis runs over, the one named last changes fastest.
Arguments:
- gradients: bfloat16 [32768, 128], P('rows'), may hold values from -6 to 6
- hessians: bfloat16 [32768], P('rows'), may hold values from 0.25 to 2
- bin_words: int32 [128, 32768], P('feat', 'rows'), may hold values from 0 to 4095, as said below
- children: int32 [3, 32768], P(None, 'rows'), may hold values from 0 to 1, as said below
- split_feature: int32 [14], replicated, may hold values from 0 to 255
- split_bin: int32 [14], replicated, may hold values from 0 to 62
Outputs:
- split_gain_one: float32 [128, 256], P('rows', 'feat')
- split_gain_two: float32 [256, 256], P('rows', 'feat')
- split_gain_three: float32 [512, 256], P('rows', 'feat')
- child_scores: float32 [3, 64, 2, 128], P(None, 'rows')
Inputs may be any that keep to these rules, and one draw needn't show every extreme that they name: `children`: of the 512 rows of one device, at most 3 / 4, 1 / 2 and 1 / 4 of 512 lie in one node at depths 1, 2 and 3; every device reaches each of these bounds in some node. `bin_words`: word w of panel p, six bits a feature with the lowest bits first, holds the bins of the panel's features 2 w and 2 w + 1, numbered within the panel of 64 features; slots past the panel's last feature are zero. Every bin is below 64.
All inputs are finite; a program needn't handle non-finite values.
Results may differ from a plain program's by a relative error of at most 0.0003.
Values may be sent and summed in bfloat16 or wider, within the bound.
A program may use at most 64 MiB of HBM per device.

v0:
```python
import jax
import jax.numpy as jnp
from jax import lax
from jax.sharding import PartitionSpec as P

FEATURES = 256
BINS = 64
OUT = 128
LEVELS = 3
penalty = 1.0


def as_sent(array):
    return jax.tree.map(lambda a: a.astype(jnp.bfloat16) if a.dtype == jnp.float32 else a, array)


def swapped(block, axis, stride):
    count = lax.axis_size(axis)
    route = []
    for low in range(count):
        high = low | 1 << stride
        if high != low and high < count:
            route += [(low, high), (high, low)]
    return lax.ppermute(block, axis, route)


def unpack_codes(packed):
    shifts = 6 * jnp.arange(2, dtype=jnp.int32)
    pieces = jnp.bitwise_and(jnp.right_shift(packed[:, None, :], shifts[None, :, None]), 63)
    return pieces.reshape(-1, packed.shape[-1])


def split_terms(cumulative, hess_cum):
    total_sum = cumulative[..., -1:, :]
    hess_total = hess_cum[..., -1:]
    right_sum = total_sum - cumulative
    hess_right = hess_total - hess_cum
    split_score = (
        jnp.sum(cumulative * cumulative, -1) / (hess_cum + penalty)
        + jnp.sum(right_sum * right_sum, -1) / (hess_right + penalty)
        - jnp.sum(total_sum * total_sum, -1) / (hess_total + penalty)
    ) / OUT
    return (split_score, right_sum, hess_right)


def front_index(marked, slot_total):
    running = jnp.cumsum(marked.astype(jnp.int32))
    wanted = jnp.arange(slot_total, dtype=jnp.int32) + 1
    source = jnp.searchsorted(running, wanted, side="left")
    filled = wanted <= running[-1]
    return (jnp.minimum(source, marked.shape[0] - 1), filled)


def pick_rows(values, source, filled):
    taken = jnp.take(values, source, axis=0)
    return jnp.where(filled[:, None], taken, jnp.zeros_like(taken))


def pick_slots(values, source, filled):
    taken = jnp.take(values, source, axis=0)
    return jnp.where(filled, taken, jnp.zeros_like(taken))


def pick_columns(values, source, filled):
    taken = jnp.take(values, source, axis=1)
    return jnp.where(filled[None, :], taken, jnp.zeros_like(taken))


def build_hist(bin_codes, grad_rows, hess_rows, block_rows):
    feat_count = bin_codes.shape[0]
    bin_levels = jnp.arange(BINS, dtype=jnp.int32)

    def add_block(step_index, running):
        start_row = step_index * block_rows
        code_block = lax.dynamic_slice_in_dim(bin_codes, start_row, block_rows, 1)
        grad_block = lax.dynamic_slice_in_dim(grad_rows, start_row, block_rows, 0)
        hess_block = lax.dynamic_slice_in_dim(hess_rows, start_row, block_rows, 0)
        one_hot = (code_block[:, None, :] == bin_levels[None, :, None]).astype(jnp.bfloat16)
        one_hot = one_hot.reshape(feat_count * BINS, block_rows)
        return (
            running[0] + jnp.dot(one_hot, grad_block, preferred_element_type=jnp.float32),
            running[1] + jnp.dot(one_hot, hess_block, preferred_element_type=jnp.float32),
        )

    initial = (
        jnp.zeros((feat_count * BINS, OUT), jnp.float32),
        jnp.zeros((feat_count * BINS,), jnp.float32),
    )
    return lax.fori_loop(0, grad_rows.shape[0] // block_rows, add_block, initial)


def on_device(gradients, hessians, bin_words, children, split_feature, split_bin):
    row_count = lax.axis_size("rows")
    top_bit = row_count.bit_length() - 1
    row_index = lax.axis_index("rows")
    panel_index = lax.axis_index("feat")
    feat_dev = FEATURES // lax.axis_size("feat")
    row_dev = gradients.shape[0]
    slot_count = 2 * row_dev
    block_rows = min(256, slot_count)
    pad_rows = slot_count - row_dev
    grad_rows = jnp.concatenate([gradients, jnp.zeros((pad_rows, OUT), jnp.bfloat16)], 0)
    hess_rows = jnp.concatenate([hessians, jnp.zeros((pad_rows,), jnp.bfloat16)], 0)
    word_rows = jnp.concatenate(
        [bin_words, jnp.zeros((bin_words.shape[0], pad_rows), jnp.int32)], 1
    )
    child_rows = jnp.concatenate([children, jnp.zeros((children.shape[0], pad_rows), jnp.int32)], 1)
    splits_total = split_feature.shape[0]
    collected = jnp.zeros((splits_total, 2, OUT), jnp.float32)
    gain_list = []
    slot_list = []
    for level_index in range(LEVELS):
        cross_bit = top_bit - 1 - level_index
        half_bit = jnp.bitwise_and(jnp.right_shift(row_index, cross_bit), 1)
        living = hess_rows > 0
        staying = living & (child_rows[level_index] == half_bit)
        leaving = living & (child_rows[level_index] != half_bit)
        sent_hess = jnp.where(leaving, hess_rows, jnp.zeros_like(hess_rows))
        got_grad, got_hess, got_words, got_child = (
            swapped(grad_rows, "rows", cross_bit),
            swapped(sent_hess, "rows", cross_bit),
            swapped(as_sent(word_rows), "rows", cross_bit).astype(word_rows.dtype),
            swapped(as_sent(child_rows), "rows", cross_bit).astype(child_rows.dtype),
        )
        accepted = jnp.concatenate([staying, got_hess > 0])
        source, filled = front_index(accepted, slot_count)
        grad_rows = pick_rows(jnp.concatenate([grad_rows, got_grad], 0), source, filled)
        hess_rows = pick_slots(jnp.concatenate([hess_rows, got_hess], 0), source, filled)
        word_rows = pick_columns(jnp.concatenate([word_rows, got_words], 1), source, filled)
        child_rows = pick_columns(jnp.concatenate([child_rows, got_child], 1), source, filled)
        bin_codes = unpack_codes(word_rows)
        hist_grad, hist_hess = build_hist(bin_codes, grad_rows, hess_rows, block_rows)
        group_size = row_count >> level_index + 1
        node_count = 2 ** (level_index + 1)
        node_here = jnp.right_shift(row_index, top_bit - level_index - 1)
        share_grad = hist_grad.reshape(feat_dev, BINS * OUT)
        share_hess = hist_hess.reshape(feat_dev, BINS)
        for step_bit in reversed(range(top_bit - level_index - 1)):
            half_rows = share_grad.shape[0] // 2
            upper_half = jnp.bitwise_and(jnp.right_shift(row_index, step_bit), 1) == 1
            keep_grad = jnp.where(upper_half, share_grad[half_rows:], share_grad[:half_rows])
            give_grad = jnp.where(upper_half, share_grad[:half_rows], share_grad[half_rows:])
            keep_hess = jnp.where(upper_half, share_hess[half_rows:], share_hess[:half_rows])
            give_hess = jnp.where(upper_half, share_hess[:half_rows], share_hess[half_rows:])
            got_partial, got_curv = swapped((give_grad, give_hess), "rows", step_bit)
            share_grad = keep_grad + got_partial
            share_hess = keep_hess + got_curv
        share_count = share_grad.shape[0]
        cumulative = jnp.cumsum(share_grad.reshape(share_count, BINS, OUT), axis=1)
        hess_cum = jnp.cumsum(share_hess, axis=1)
        split_score, right_sum, hess_right = split_terms(cumulative, hess_cum)
        gain_list.append(split_score)
        position = jnp.bitwise_and(row_index, group_size - 1)
        split_slot = node_count - 2 + node_here
        feature_id = split_feature[split_slot]
        bin_id = split_bin[split_slot]
        inner_feature = feature_id % feat_dev
        is_owner = (feature_id // feat_dev == panel_index) & (
            inner_feature // share_count == position
        )
        chosen = (
            (jnp.arange(share_count)[:, None] == inner_feature % share_count)
            & (jnp.arange(BINS)[None, :] == bin_id)
            & is_owner
        )
        left_grad = jnp.sum(jnp.where(chosen[..., None], cumulative, 0.0), axis=(0, 1))
        left_hess = jnp.sum(jnp.where(chosen, hess_cum, 0.0))
        right_grad = jnp.sum(jnp.where(chosen[..., None], right_sum, 0.0), axis=(0, 1))
        right_hess = jnp.sum(jnp.where(chosen, hess_right, 0.0))
        child_pair = jnp.stack(
            [
                -left_grad / jnp.sqrt(left_hess + penalty),
                -right_grad / jnp.sqrt(right_hess + penalty),
            ],
            0,
        )
        slot_match = jnp.arange(splits_total) == split_slot
        collected = collected + jnp.where(slot_match[:, None, None], child_pair[None], 0.0)
        slot_list.append(split_slot)
    totals = lax.psum(collected, ("rows", "feat"))
    child_scores = jnp.stack([totals[slot_index] for slot_index in slot_list], 0)[:, None]
    return (gain_list[0], gain_list[1], gain_list[2], child_scores)


def solution(mesh):
    placed = (P("rows", None), P("rows"), P("feat", "rows"), P(None, "rows"), P(), P())
    return jax.shard_map(
        on_device,
        mesh=mesh,
        in_specs=placed,
        out_specs=(
            P("rows", "feat"),
            P("rows", "feat"),
            P("rows", "feat"),
            P(None, "rows", None, None),
        ),
        check_vma=False,
    )
```

profile of v0, /device:TPU:1, one launch (start us, length us, event | category | flops | bytes accessed | tf_op | source)
XLA Modules:
  0.0 707.1 jit_solution(15301522432196689266)
XLA Ops:
  22.0 74.8 %while.98 = (s32[]{:T(128)}, u32[1024]{0:T(1024)S(1)}, u32[1024]{0:T(1024)S(1)}, s32[2048]{0:T(1024)S(1)}, s32[]{:T(128)}, /*index=5*/s32[]{:T(128)}, s32[]{}) while((s32[]{:T(128)}, u32[1024]{0:T(1024)S(1)}, u32[1024]{0:T(1024)S(1)}, s32[2048]{0:T(1024)S(1)}, s32[]{:T(128)}, /*index=5*/s32[]{:T(128)}, s32[]{}) %tuple.223), condition=%wide.region_3.4_spmd.clone, body=%wide.region_2.3_spmd.clone.sunk | while | flops 20484 | bytes 63589 | solution.py:49
  22.0 6.2 gather_fusion
  28.3 6.2 gather_fusion
  34.5 6.2 gather_fusion
  40.7 6.2 gather_fusion
  47.0 6.2 gather_fusion
  53.2 6.2 gather_fusion
  59.4 6.2 gather_fusion
  65.7 6.2 gather_fusion
  78.1 6.2 gather_fusion
  84.4 6.2 gather_fusion
  90.6 6.2 gather_fusion
  97.5 6.8 gather_fusion.5
  112.2 74.8 %while.100 = (s32[]{:T(128)}, u32[1024]{0:T(1024)S(1)}, u32[1024]{0:T(1024)S(1)}, s32[2048]{0:T(1024)S(1)}, s32[]{:T(128)}, /*index=5*/s32[]{:T(128)}, s32[]{}) while((s32[]{:T(128)}, u32[1024]{0:T(1024)S(1)}, u32[1024]{0:T(1024)S(1)}, s32[2048]{0:T(1024)S(1)}, s32[]{:T(128)}, /*index=5*/s32[]{:T(128)}, s32[]{}) %tuple.226), condition=%wide.region_14.19_spmd.clone, body=%wide.region_13.18_spmd.clone.sunk | while | flops 20484 | bytes 63589 | solution.py:49
  124.7 6.2 gather_fusion.1
  188.3 6.8 gather_fusion.9
  199.6 7.0 collective-permute-start.26
  210.8 74.8 %while.102 = (s32[]{:T(128)}, u32[1024]{0:T(1024)S(1)}, u32[1024]{0:T(1024)S(1)}, s32[2048]{0:T(1024)S(1)}, s32[]{:T(128)}, /*index=5*/s32[]{:T(128)}, s32[]{}) while((s32[]{:T(128)}, u32[1024]{0:T(1024)S(1)}, u32[1024]{0:T(1024)S(1)}, s32[2048]{0:T(1024)S(1)}, s32[]{:T(128)}, /*index=5*/s32[]{:T(128)}, s32[]{}) %tuple.229), condition=%wide.region_25.30_spmd.clone, body=%wide.region_24.29_spmd.clone.sunk | while | flops 20484 | bytes 63589 | solution.py:49
  286.2 6.8 gather_fusion.13
  325.9 10.0 %collective-permute-done.27 = s32[32,1024]{0,1:T(8,128)} collective-permute-done((s32[32,1024]{0,1:T(8,128)S(1)}, s32[32,1024]{0,1:T(8,128)}, u32[]{:S(2)}, u32[]{:S(2)}) %collective-permute-start.27) | collective-permute-done | bytes 131104 | tf_op jit(solution)/shard_map/ppermute | solution.py:24
  347.7 14.4 %while.99 = (s32[]{:T(128)}, f32[4096,128]{1,0:T(8,128)S(1)}, f32[4096]{0:T(1024)S(1)}, s32[64,1024]{1,0:T(8,128)}, bf16[1024,128]{1,0:T(8,128)(2,1)S(1)}, /*ind...) while((s32[]{:T(128)}, f32[4096,128]{1,0:T(8,128)S(1)}, ...), condition=%wide.region_5.9_spmd.clone, body=%wide.region_4.8_spmd.clone.sunk | while | flops 272637952 | bytes 7735978 | solution.py:89
  371.3 8.6 %collective-permute-start.10 = (f32[8,64]{1,0:T(8,128)S(1)}, f32[8,64]{1,0:T(8,128)S(1)}, u32[]{:S(2)}, u32[]{:S(2)}) collective-permute-start(f32[8,64]{1,0:T(8,128)S(1)} %slice_select_fusion.26), channel_id=1, source_target_pairs={{0,16},{16,0},{4,20},{20,4},{8,24},{24,8},{12,28},{28,12},{32,48},... | collective-permute-start | bytes 6152 | tf_op jit(solution)/shard_map/ppermute | solution.py:24
  395.3 22.7 %while.101 = (s32[]{:T(128)}, f32[4096,128]{1,0:T(8,128)}, f32[4096]{0:T(1024)S(1)}, s32[64,1024]{1,0:T(8,128)}, bf16[1024,128]{1,0:T(8,128)(2,1)S(1)}, /*index=...) while((s32[]{:T(128)}, f32[4096,128]{1,0:T(8,128)}, ...), condition=%wide.region_16.21_spmd.clone, body=%wide.region_15.20_spmd.clone.sunk | while | flops 272637952 | bytes 7735978 | solution.py:89
  420.2 6.4 collective-permute-start.12
  448.5 17.1 %while.103 = (s32[]{:T(128)}, f32[4096,128]{1,0:T(8,128)S(1)}, f32[4096]{0:T(1024)S(1)}, s32[64,1024]{1,0:T(8,128)}, bf16[1024,128]{1,0:T(8,128)(2,1)S(1)}, /*in...) while((s32[]{:T(128)}, f32[4096,128]{1,0:T(8,128)S(1)}, ...), condition=%wide.region_27.32_spmd.clone, body=%wide.region_26.31_spmd.clone.sunk | while | flops 272637952 | bytes 7735978 | solution.py:89
  465.8 7.1 %collective-permute-start.24 = (f32[4,64]{1,0:T(4,128)S(1)}, f32[4,64]{1,0:T(4,128)S(1)}, u32[]{:S(2)}, u32[]{:S(2)}) collective-permute-start(f32[4,64]{1,0:T(4,128)S(1)} %slice_select_fusion.27), channel_id=1, source_target_pairs={{0,4},{4,0},{8,12},{12,8},{16,20},{20,16},{24,28},{28,24},{32,36},... | collective-permute-start | bytes 3080 | tf_op jit(solution)/shard_map/ppermute | solution.py:24
  472.9 18.8 %collective-permute-done.32 = f32[32,64]{1,0:T(8,128)S(1)} collective-permute-done((f32[32,64]{1,0:T(8,128)S(1)}, f32[32,64]{1,0:T(8,128)S(1)}, u32[]{:S(2)}, u32[]{:S(2)}) %collective-permute-start.32) | collective-permute-done | bytes 8224 | tf_op jit(solution)/shard_map/ppermute | solution.py:24
  508.4 73.3 %collective-permute-done.29 = f32[32,8192]{1,0:T(8,128)} collective-permute-done((f32[32,8192]{1,0:T(8,128)}, f32[32,8192]{1,0:T(8,128)}, u32[]{:S(2)}, u32[]{:S(2)}) %collective-permute-start.29) | collective-permute-done | bytes 1048608 | tf_op jit(solution)/shard_map/ppermute | solution.py:24
  585.3 7.6 %collective-permute-done.18 = f32[16,8192]{1,0:T(8,128)S(1)} collective-permute-done((f32[16,8192]{1,0:T(8,128)S(1)}, f32[16,8192]{1,0:T(8,128)S(1)}, u32[]{:S(2)}, u32[]{:S(2)}) %collective-permute-start.18) | collective-permute-done | bytes 524320 | tf_op jit(solution)/shard_map/ppermute | solution.py:24
  592.9 11.2 %collective-permute-done.5 = f32[8,8192]{1,0:T(8,128)S(1)} collective-permute-done((f32[8,8192]{1,0:T(8,128)S(1)}, f32[8,8192]{1,0:T(8,128)S(1)}, u32[]{:S(2)}, u32[]{:S(2)}) %collective-permute-start.5) | collective-permute-done | bytes 262176 | tf_op jit(solution)/shard_map/ppermute | solution.py:24
  606.1 6.3 collective-permute-done.6
  629.2 76.1 %psum.7 = f32[14,2,128]{2,1,0:T(2,128)S(1)} all-reduce(f32[14,2,128]{2,1,0:T(2,128)S(1)} %select_add_fusion.9), channel_id=1, replica_groups=mesh['rows'=64,'feat'=4] {'rows','feat'}, use_global_device_ids=true, to_apply=%region_45.50 | all-reduce | flops 3584 | bytes 28672 | tf_op jit(solution)/shard_map/psum | solution.py:180
  (588 shorter events, 364.7 us)
Async XLA Ops:
  2.1 18.7 %collective-permute-start = (bf16[1024]{0:T(1024)(128)(2,1)S(1)}, bf16[1024]{0:T(1024)(128)(2,1)S(1)}, u32[]{:S(2)}, u32[]{:S(2)}) collective-permute-start(bf16[1024]{0:T(1024)(128)(2,1)S(1)} %and_select_fusion.2), channel_id=1, source_target_pairs={{0,128},{128,0},{4,132},{132,4},{8,136},{136,8},{12,140},{140,12},... | collective-permute-start | bytes 6152 | tf_op jit(solution)/shard_map/ppermute | solution.py:24
  6.6 97.8 %collective-permute-start.13 = (s32[3,1024]{1,0:T(4,128)S(1)}, s32[3,1024]{1,0:T(4,128)S(1)}, u32[]{:S(2)}, u32[]{:S(2)}) collective-permute-start(s32[3,1024]{1,0:T(4,128)S(1)} %concatenate.74), channel_id=1, source_target_pairs={{0,128},{128,0},{4,132},{132,4},{8,136},{136,8},{12,140},{140,12},... | collective-permute-start | bytes 36872 | tf_op jit(solution)/shard_map/ppermute | solution.py:24
  7.4 285.6 %collective-permute-start.1 = (s32[32,1024]{1,0:T(8,128)S(1)}, s32[32,1024]{1,0:T(8,128)S(1)}, u32[]{:S(2)}, u32[]{:S(2)}) collective-permute-start(s32[32,1024]{1,0:T(8,128)S(1)} %concatenate.78), channel_id=1, source_target_pairs={{0,128},{128,0},{4,132},{132,4},{8,136},{136,8},{12,140},{140,12},... | collective-permute-start | bytes 393224 | tf_op jit(solution)/shard_map/ppermute | solution.py:24
  12.1 306.9 %collective-permute-start.2 = (bf16[1024,128]{1,0:T(8,128)(2,1)}, bf16[1024,128]{1,0:T(8,128)(2,1)}, u32[]{:S(2)}, u32[]{:S(2)}) collective-permute-start(bf16[1024,128]{1,0:T(8,128)(2,1)} %concatenate.80), channel_id=1, source_target_pairs={{0,128},{128,0},{4,132},{132,4},{8,136},{136,8},{12,140},{140,12},... | collective-permute-start | bytes 786440 | tf_op jit(solution)/shard_map/ppermute | solution.py:24
  111.1 84.0 %collective-permute-start.25 = (s32[3,1024]{0,1:T(8,128)S(1)}, s32[3,1024]{0,1:T(8,128)S(1)}, u32[]{:S(2)}, u32[]{:S(2)}) collective-permute-start(s32[3,1024]{0,1:T(8,128)S(1)} %bitcast_select_fusion.2), channel_id=1, source_target_pairs={{0,64},{64,0},{4,68},{68,4},{8,72},{72,8},{12,76},{76,12},{16,80},... | collective-permute-start | bytes 36872 | tf_op jit(solution)/shard_map/ppermute | solution.py:24
  199.6 10.6 %collective-permute-start.26 = (bf16[1024]{0:T(1024)(128)(2,1)S(1)}, bf16[1024]{0:T(1024)(128)(2,1)S(1)}, u32[]{:S(2)}, u32[]{:S(2)}) collective-permute-start(bf16[1024]{0:T(1024)(128)(2,1)S(1)} %and_select_fusion), channel_id=1, source_target_pairs={{0,32},{32,0},{4,36},{36,4},{8,40},{40,8},{12,44},{44,12},{16,48},... | collective-permute-start | bytes 6152 | tf_op jit(solution)/shard_map/ppermute | solution.py:24
  298.8 10.4 %collective-permute-start.15 = (s32[32,1024]{0,1:T(8,128)S(1)}, s32[32,1024]{0,1:T(8,128)}, u32[]{:S(2)}, u32[]{:S(2)}) collective-permute-start(s32[32,1024]{0,1:T(8,128)S(1)} %bitcast_select_fusion.3), channel_id=1, source_target_pairs={{0,64},{64,0},{4,68},{68,4},{8,72},{72,8},{12,76},{76,12},{16,80},... | collective-permute-start | bytes 393224 | tf_op jit(solution)/shard_map/ppermute | solution.py:24
  315.7 20.2 %collective-permute-start.27 = (s32[32,1024]{0,1:T(8,128)S(1)}, s32[32,1024]{0,1:T(8,128)}, u32[]{:S(2)}, u32[]{:S(2)}) collective-permute-start(s32[32,1024]{0,1:T(8,128)S(1)} %bitcast_select_fusion.1), channel_id=1, source_target_pairs={{0,32},{32,0},{4,36},{36,4},{8,40},{40,8},{12,44},{44,12},{16,48},... | collective-permute-start | bytes 393224 | tf_op jit(solution)/shard_map/ppermute | solution.py:24
  364.8 6.5 collective-permute-start.9
  371.3 9.9 %collective-permute-start.10 = (f32[8,64]{1,0:T(8,128)S(1)}, f32[8,64]{1,0:T(8,128)S(1)}, u32[]{:S(2)}, u32[]{:S(2)}) collective-permute-start(f32[8,64]{1,0:T(8,128)S(1)} %slice_select_fusion.26), channel_id=1, source_target_pairs={{0,16},{16,0},{4,20},{20,4},{8,24},{24,8},{12,28},{28,12},{32,48},... | collective-permute-start | bytes 6152 | tf_op jit(solution)/shard_map/ppermute | solution.py:24
  379.9 10.8 %collective-permute-start.16 = (bf16[1024,128]{1,0:T(8,128)(2,1)S(1)}, bf16[1024,128]{1,0:T(8,128)(2,1)}, u32[]{:S(2)}, u32[]{:S(2)}) collective-permute-start(bf16[1024,128]{1,0:T(8,128)(2,1)S(1)} %get-tuple-element.1187), channel_id=1, source_target_pairs={{0,64},{64,0},{4,68},{68,4},{8,72},{72,8},{12,76},{76,12},{16,80},... | collective-permute-start | bytes 786440 | tf_op jit(solution)/shard_map/ppermute | solution.py:24
  381.2 9.5 %collective-permute-start.11 = (f32[4,64]{1,0:T(4,128)S(1)}, f32[4,64]{1,0:T(4,128)S(1)}, u32[]{:S(2)}, u32[]{:S(2)}) collective-permute-start(f32[4,64]{1,0:T(4,128)S(1)} %slice_select_fusion.28), channel_id=1, source_target_pairs={{0,8},{8,0},{4,12},{12,4},{16,24},{24,16},{20,28},{28,20},{32,40},... | collective-permute-start | bytes 3080 | tf_op jit(solution)/shard_map/ppermute | solution.py:24
  388.2 112.1 %collective-permute-start.3 = (f32[32,8192]{1,0:T(8,128)}, f32[32,8192]{1,0:T(8,128)}, u32[]{:S(2)}, u32[]{:S(2)}) collective-permute-start(f32[32,8192]{1,0:T(8,128)} %select_n.551), channel_id=1, source_target_pairs={{0,64},{64,0},{4,68},{68,4},{8,72},{72,8},{12,76},{76,12},{16,80},... | collective-permute-start | bytes 3145736 | tf_op jit(solution)/shard_map/ppermute | solution.py:24
  418.1 8.6 %collective-permute-start.21 = (f32[32,64]{1,0:T(8,128)S(1)}, f32[32,64]{1,0:T(8,128)S(1)}, u32[]{:S(2)}, u32[]{:S(2)}) collective-permute-start(f32[32,64]{1,0:T(8,128)S(1)} %select_n.603), channel_id=1, source_target_pairs={{0,32},{32,0},{4,36},{36,4},{8,40},{40,8},{12,44},{44,12},{16,48},... | collective-permute-start | bytes 24584 | tf_op jit(solution)/shard_map/ppermute | solution.py:24
  420.2 7.2 %collective-permute-start.12 = (f32[2,64]{1,0:T(2,128)S(1)}, f32[2,64]{1,0:T(2,128)S(1)}, u32[]{:S(2)}, u32[]{:S(2)}) collective-permute-start(f32[2,64]{1,0:T(2,128)S(1)} %broadcast_select_fusion.1), channel_id=1, source_target_pairs={{0,4},{4,0},{8,12},{12,8},{16,20},{20,16},{24,28},{28,24},{32,36},... | collective-permute-start | bytes 1544 | tf_op jit(solution)/shard_map/ppermute | solution.py:24
  426.7 4.5 collective-permute-start.22
  427.7 16.2 %collective-permute-start.28 = (bf16[1024,128]{1,0:T(8,128)(2,1)S(1)}, bf16[1024,128]{1,0:T(8,128)(2,1)}, u32[]{:S(2)}, u32[]{:S(2)}) collective-permute-start(bf16[1024,128]{1,0:T(8,128)(2,1)S(1)} %get-tuple-element.1189), channel_id=1, source_target_pairs={{0,32},{32,0},{4,36},{36,4},{8,40},{40,8},{12,44},{44,12},{16,48},... | collective-permute-start | bytes 786440 | tf_op jit(solution)/shard_map/ppermute | solution.py:24
  431.2 12.7 %collective-permute-start.23 = (f32[8,64]{1,0:T(8,128)S(1)}, f32[8,64]{1,0:T(8,128)S(1)}, u32[]{:S(2)}, u32[]{:S(2)}) collective-permute-start(f32[8,64]{1,0:T(8,128)S(1)} %slice_select_fusion.25), channel_id=1, source_target_pairs={{0,8},{8,0},{4,12},{12,4},{16,24},{24,16},{20,28},{28,20},{32,40},... | collective-permute-start | bytes 6152 | tf_op jit(solution)/shard_map/ppermute | solution.py:24
  437.7 67.3 %collective-permute-start.17 = (f32[32,8192]{1,0:T(8,128)}, f32[32,8192]{1,0:T(8,128)}, u32[]{:S(2)}, u32[]{:S(2)}) collective-permute-start(f32[32,8192]{1,0:T(8,128)} %select_n.589), channel_id=1, source_target_pairs={{0,32},{32,0},{4,36},{36,4},{8,40},{40,8},{12,44},{44,12},{16,48},... | collective-permute-start | bytes 3145736 | tf_op jit(solution)/shard_map/ppermute | solution.py:24
  465.7 26.0 %collective-permute-start.32 = (f32[32,64]{1,0:T(8,128)S(1)}, f32[32,64]{1,0:T(8,128)S(1)}, u32[]{:S(2)}, u32[]{:S(2)}) collective-permute-start(f32[32,64]{1,0:T(8,128)S(1)} %select_n.632), channel_id=1, source_target_pairs={{0,16},{16,0},{4,20},{20,4},{8,24},{24,8},{12,28},{28,12},{32,48},... | collective-permute-start | bytes 24584 | tf_op jit(solution)/shard_map/ppermute | solution.py:24
  465.8 26.0 %collective-permute-start.24 = (f32[4,64]{1,0:T(4,128)S(1)}, f32[4,64]{1,0:T(4,128)S(1)}, u32[]{:S(2)}, u32[]{:S(2)}) collective-permute-start(f32[4,64]{1,0:T(4,128)S(1)} %slice_select_fusion.27), channel_id=1, source_target_pairs={{0,4},{4,0},{8,12},{12,8},{16,20},{20,16},{24,28},{28,24},{32,36},... | collective-permute-start | bytes 3080 | tf_op jit(solution)/shard_map/ppermute | solution.py:24
  494.3 5.8 collective-permute-start.34
  499.5 82.2 %collective-permute-start.29 = (f32[32,8192]{1,0:T(8,128)}, f32[32,8192]{1,0:T(8,128)}, u32[]{:S(2)}, u32[]{:S(2)}) collective-permute-start(f32[32,8192]{1,0:T(8,128)} %select_n.621), channel_id=1, source_target_pairs={{0,16},{16,0},{4,20},{20,4},{8,24},{24,8},{12,28},{28,12},{32,48},... | collective-permute-start | bytes 3145736 | tf_op jit(solution)/shard_map/ppermute | solution.py:24
  501.8 81.4 %collective-permute-start.4 = (f32[16,8192]{1,0:T(8,128)S(1)}, f32[16,8192]{1,0:T(8,128)S(1)}, u32[]{:S(2)}, u32[]{:S(2)}) collective-permute-start(f32[16,8192]{1,0:T(8,128)S(1)} %slice_select_fusion.9), channel_id=1, source_target_pairs={{0,32},{32,0},{4,36},{36,4},{8,40},{40,8},{12,44},{44,12},{16,48},... | collective-permute-start | bytes 1572872 | tf_op jit(solution)/shard_map/ppermute | solution.py:24
  506.4 86.4 %collective-permute-start.18 = (f32[16,8192]{1,0:T(8,128)S(1)}, f32[16,8192]{1,0:T(8,128)S(1)}, u32[]{:S(2)}, u32[]{:S(2)}) collective-permute-start(f32[16,8192]{1,0:T(8,128)S(1)} %slice_select_fusion.8), channel_id=1, source_target_pairs={{0,16},{16,0},{4,20},{20,4},{8,24},{24,8},{12,28},{28,12},{32,48},... | collective-permute-start | bytes 1572872 | tf_op jit(solution)/shard_map/ppermute | solution.py:24
  583.0 35.7 %collective-permute-start.30 = (f32[16,8192]{1,0:T(8,128)S(1)}, f32[16,8192]{1,0:T(8,128)S(1)}, u32[]{:S(2)}, u32[]{:S(2)}) collective-permute-start(f32[16,8192]{1,0:T(8,128)S(1)} %slice_select_fusion.7), channel_id=1, source_target_pairs={{0,8},{8,0},{4,12},{12,4},{16,24},{24,16},{20,28},{28,20},{32,40},... | collective-permute-start | bytes 1572872 | tf_op jit(solution)/shard_map/ppermute | solution.py:24
  583.3 20.8 %collective-permute-start.5 = (f32[8,8192]{1,0:T(8,128)S(1)}, f32[8,8192]{1,0:T(8,128)S(1)}, u32[]{:S(2)}, u32[]{:S(2)}) collective-permute-start(f32[8,8192]{1,0:T(8,128)S(1)} %slice_select_fusion.12), channel_id=1, source_target_pairs={{0,16},{16,0},{4,20},{20,4},{8,24},{24,8},{12,28},{28,12},{32,48},... | collective-permute-start | bytes 786440 | tf_op jit(solution)/shard_map/ppermute | solution.py:24
  604.2 8.2 %collective-permute-start.6 = (f32[4,8192]{1,0:T(4,128)S(1)}, f32[4,8192]{1,0:T(4,128)S(1)}, u32[]{:S(2)}, u32[]{:S(2)}) collective-permute-start(f32[4,8192]{1,0:T(4,128)S(1)} %slice_select_fusion.14), channel_id=1, source_target_pairs={{0,8},{8,0},{4,12},{12,4},{16,24},{24,16},{20,28},{28,20},{32,40},... | collective-permute-start | bytes 393224 | tf_op jit(solution)/shard_map/ppermute | solution.py:24
  604.6 13.4 %collective-permute-start.19 = (f32[8,8192]{1,0:T(8,128)S(1)}, f32[8,8192]{1,0:T(8,128)S(1)}, u32[]{:S(2)}, u32[]{:S(2)}) collective-permute-start(f32[8,8192]{1,0:T(8,128)S(1)} %slice_select_fusion.11), channel_id=1, source_target_pairs={{0,8},{8,0},{4,12},{12,4},{16,24},{24,16},{20,28},{28,20},{32,40},... | collective-permute-start | bytes 786440 | tf_op jit(solution)/shard_map/ppermute | solution.py:24
  612.5 6.5 collective-permute-start.7
  618.1 4.3 collective-permute-start.20
  618.9 7.2 %collective-permute-start.31 = (f32[8,8192]{1,0:T(8,128)S(1)}, f32[8,8192]{1,0:T(8,128)S(1)}, u32[]{:S(2)}, u32[]{:S(2)}) collective-permute-start(f32[8,8192]{1,0:T(8,128)S(1)} %slice_select_fusion.10), channel_id=1, source_target_pairs={{0,4},{4,0},{8,12},{12,8},{16,20},{20,16},{24,28},{28,24},{32,36},... | collective-permute-start | bytes 786440 | tf_op jit(solution)/shard_map/ppermute | solution.py:24
  (24 other events, 253.7 us)
where the time goes:
time: 718 us; the launch traced here: 707 us
  local copies, waits for them, and re-layouts  310 us (43%)
  waiting for transfers between devices  148 us (21%)
  blocking collectives  76.1 us (11%)
  starting transfers between devices  69.2 us (10%)
  other arithmetic  58 us (8%)
  matrix products  30.3 us (4%)
  between operations  13.7 us (2%)
    gather x36, local copies, waits for them, and re-layouts, front_index(): source = jnp.searchsorted(running, wanted, side='left')  222 us
    ppermute x35, waiting for transfers between devices, swapped(): return lax.ppermute(block, axis, route)  148 us
    psum x1, blocking collectives, on_device(): totals = lax.psum(collected, ('rows', 'feat'))  76.1 us
    ppermute x35, starting transfers between devices, swapped(): return lax.ppermute(block, axis, route)  69.2 us
    dot_general x12, matrix products, add_block(): jnp.dot(one_hot, grad_block, preferred_element_type=jnp.float32)  22.6 us
    gather x3, local copies, waits for them, and re-layouts, pick_slots(): taken = jnp.take(values, source, axis=0)  20.4 us
    gather x5, local copies, waits for them, and re-layouts, pick_columns(): taken = jnp.take(values, source, axis=1)  19 us
  transfers between devices with their start and end apart: 35, of which 14 were waited for; matrix products, arithmetic and copies ran while one was open for 52% of the time, Pallas kernels for 0%

commit v1 on v0

--- a/solution.py
+++ b/solution.py
@@ -177,7 +177,9 @@
         slot_match = jnp.arange(splits_total) == split_slot
         collected = collected + jnp.where(slot_match[:, None, None], child_pair[None], 0.0)
         slot_list.append(split_slot)
-    totals = lax.psum(collected, ("rows", "feat"))
+    totals = collected
+    for mesh_axis in ("rows", "feat"):
+        totals = lax.psum(totals, mesh_axis)
     child_scores = jnp.stack([totals[slot_index] for slot_index in slot_list], 0)[:, None]
     return (gain_list[0], gain_list[1], gain_list[2], child_scores)
 

time: 718 us -> 905 us (1.26)
  blocking collectives: 76.1 us -> 258 us
    psum x1 -> x2, blocking collectives: 76.1 us -> 258 us  [on_device(): totals = lax.psum(totals, mesh_axis)]
  transfers between devices with their start and end apart: 35 -> 35, of which waited for: 14 -> 14; matrix products, arithmetic and copies ran while one was open for 52% -> 41% of each run, Pallas kernels for 0% -> 0%
where the time goes in v1:
time: 905 us; the launch traced here: 889 us
  local copies, waits for them, and re-layouts  310 us (34%)
  blocking collectives  258 us (29%)
  waiting for transfers between devices  148 us (16%)
  starting transfers between devices  69.2 us (8%)
  other arithmetic  58 us (6%)
  matrix products  30.3 us (3%)
  between operations  13.7 us (2%)
    psum x2, blocking collectives, on_device(): totals = lax.psum(totals, mesh_axis)  258 us
    gather x36, local copies, waits for them, and re-layouts, front_index(): source = jnp.searchsorted(running, wanted, side='left')  222 us
    ppermute x35, waiting for transfers between devices, swapped(): return lax.ppermute(block, axis, route)  148 us
    ppermute x35, starting transfers between devices, swapped(): return lax.ppermute(block, axis, route)  69.2 us
    dot_general x12, matrix products, add_block(): jnp.dot(one_hot, grad_block, preferred_element_type=jnp.float32)  22.6 us
    gather x3, local copies, waits for them, and re-layouts, pick_slots(): taken = jnp.take(values, source, axis=0)  20.4 us
    gather x5, local copies, waits for them, and re-layouts, pick_columns(): taken = jnp.take(values, source, axis=1)  19 us
  transfers between devices with their start and end apart: 35, of which 14 were waited for; matrix products, arithmetic and copies ran while one was open for 41% of the time, Pallas kernels for 0%

profile of v1, /device:TPU:1, one launch (start us, length us, event | category | flops | bytes accessed | tf_op | source)
XLA Modules:
  0.0 888.7 jit_solution(5603217316353267148)
XLA Ops:
  22.0 74.8 %while.98 = (s32[]{:T(128)}, u32[1024]{0:T(1024)S(1)}, u32[1024]{0:T(1024)S(1)}, s32[2048]{0:T(1024)S(1)}, s32[]{:T(128)}, /*index=5*/s32[]{:T(128)}, s32[]{}) while((s32[]{:T(128)}, u32[1024]{0:T(1024)S(1)}, u32[1024]{0:T(1024)S(1)}, s32[2048]{0:T(1024)S(1)}, s32[]{:T(128)}, /*index=5*/s32[]{:T(128)}, s32[]{}) %tuple.223), condition=%wide.region_3.4_spmd.clone, body=%wide.region_2.3_spmd.clone.sunk | while | flops 20484 | bytes 63589 | solution.py:49
  22.0 6.2 gather_fusion
  28.3 6.2 gather_fusion
  34.5 6.2 gather_fusion
  40.7 6.2 gather_fusion
  47.0 6.2 gather_fusion
  53.2 6.2 gather_fusion
  59.4 6.2 gather_fusion
  65.7 6.2 gather_fusion
  78.1 6.2 gather_fusion
  84.4 6.2 gather_fusion
  90.6 6.2 gather_fusion
  97.5 6.8 gather_fusion.5
  112.2 74.8 %while.100 = (s32[]{:T(128)}, u32[1024]{0:T(1024)S(1)}, u32[1024]{0:T(1024)S(1)}, s32[2048]{0:T(1024)S(1)}, s32[]{:T(128)}, /*index=5*/s32[]{:T(128)}, s32[]{}) while((s32[]{:T(128)}, u32[1024]{0:T(1024)S(1)}, u32[1024]{0:T(1024)S(1)}, s32[2048]{0:T(1024)S(1)}, s32[]{:T(128)}, /*index=5*/s32[]{:T(128)}, s32[]{}) %tuple.226), condition=%wide.region_14.19_spmd.clone, body=%wide.region_13.18_spmd.clone.sunk | while | flops 20484 | bytes 63589 | solution.py:49
  188.3 6.8 gather_fusion.9
  199.6 7.0 collective-permute-start.26
  210.8 74.8 %while.102 = (s32[]{:T(128)}, u32[1024]{0:T(1024)S(1)}, u32[1024]{0:T(1024)S(1)}, s32[2048]{0:T(1024)S(1)}, s32[]{:T(128)}, /*index=5*/s32[]{:T(128)}, s32[]{}) while((s32[]{:T(128)}, u32[1024]{0:T(1024)S(1)}, u32[1024]{0:T(1024)S(1)}, s32[2048]{0:T(1024)S(1)}, s32[]{:T(128)}, /*index=5*/s32[]{:T(128)}, s32[]{}) %tuple.229), condition=%wide.region_25.30_spmd.clone, body=%wide.region_24.29_spmd.clone.sunk | while | flops 20484 | bytes 63589 | solution.py:49
  286.2 6.8 gather_fusion.13
  325.9 10.0 %collective-permute-done.27 = s32[32,1024]{0,1:T(8,128)} collective-permute-done((s32[32,1024]{0,1:T(8,128)S(1)}, s32[32,1024]{0,1:T(8,128)}, u32[]{:S(2)}, u32[]{:S(2)}) %collective-permute-start.27) | collective-permute-done | bytes 131104 | tf_op jit(solution)/shard_map/ppermute | solution.py:24
  347.7 14.4 %while.99 = (s32[]{:T(128)}, f32[4096,128]{1,0:T(8,128)S(1)}, f32[4096]{0:T(1024)S(1)}, s32[64,1024]{1,0:T(8,128)}, bf16[1024,128]{1,0:T(8,128)(2,1)S(1)}, /*ind...) while((s32[]{:T(128)}, f32[4096,128]{1,0:T(8,128)S(1)}, ...), condition=%wide.region_5.9_spmd.clone, body=%wide.region_4.8_spmd.clone.sunk | while | flops 272637952 | bytes 7735978 | solution.py:89
  371.3 8.6 collective-permute-start.10
  395.3 22.7 %while.101 = (s32[]{:T(128)}, f32[4096,128]{1,0:T(8,128)}, f32[4096]{0:T(1024)S(1)}, s32[64,1024]{1,0:T(8,128)}, bf16[1024,128]{1,0:T(8,128)(2,1)S(1)}, /*index=...) while((s32[]{:T(128)}, f32[4096,128]{1,0:T(8,128)}, ...), condition=%wide.region_16.21_spmd.clone, body=%wide.region_15.20_spmd.clone.sunk | while | flops 272637952 | bytes 7735978 | solution.py:89
  420.2 6.4 collective-permute-start.12
  448.5 17.1 %while.103 = (s32[]{:T(128)}, f32[4096,128]{1,0:T(8,128)S(1)}, f32[4096]{0:T(1024)S(1)}, s32[64,1024]{1,0:T(8,128)}, bf16[1024,128]{1,0:T(8,128)(2,1)S(1)}, /*in...) while((s32[]{:T(128)}, f32[4096,128]{1,0:T(8,128)S(1)}, ...), condition=%wide.region_27.32_spmd.clone, body=%wide.region_26.31_spmd.clone.sunk | while | flops 272637952 | bytes 7735978 | solution.py:89
  465.8 7.1 collective-permute-start.24
  472.9 18.8 %collective-permute-done.32 = f32[32,64]{1,0:T(8,128)S(1)} collective-permute-done((f32[32,64]{1,0:T(8,128)S(1)}, f32[32,64]{1,0:T(8,128)S(1)}, u32[]{:S(2)}, u32[]{:S(2)}) %collective-permute-start.32) | collective-permute-done | bytes 8224 | tf_op jit(solution)/shard_map/ppermute | solution.py:24
  508.4 73.3 %collective-permute-done.29 = f32[32,8192]{1,0:T(8,128)} collective-permute-done((f32[32,8192]{1,0:T(8,128)}, f32[32,8192]{1,0:T(8,128)}, u32[]{:S(2)}, u32[]{:S(2)}) %collective-permute-start.29) | collective-permute-done | bytes 1048608 | tf_op jit(solution)/shard_map/ppermute | solution.py:24
  585.3 7.6 collective-permute-done.18
  592.9 11.2 %collective-permute-done.5 = f32[8,8192]{1,0:T(8,128)S(1)} collective-permute-done((f32[8,8192]{1,0:T(8,128)S(1)}, f32[8,8192]{1,0:T(8,128)S(1)}, u32[]{:S(2)}, u32[]{:S(2)}) %collective-permute-start.5) | collective-permute-done | bytes 262176 | tf_op jit(solution)/shard_map/ppermute | solution.py:24
  606.1 6.3 collective-permute-done.6
  629.2 244.3 %psum.14 = f32[14,2,128]{2,1,0:T(2,128)S(1)} all-reduce(f32[14,2,128]{2,1,0:T(2,128)S(1)} %select_add_fusion.9), channel_id=1, replica_groups=mesh['rows'=64,'feat'=4] {'rows'}, use_global_device_ids=true, to_apply=%region_45.50 | all-reduce | flops 3584 | bytes 28672 | tf_op jit(solution)/shard_map/psum | solution.py:182
  873.5 13.4 %psum.15 = f32[14,2,128]{2,1,0:T(2,128)S(1)} all-reduce(f32[14,2,128]{2,1,0:T(2,128)S(1)} %psum.14), channel_id=1, replica_groups=mesh['rows'=64,'feat'=4] {'feat'}, use_global_device_ids=true, to_apply=%region_46.51 | all-reduce | flops 3584 | bytes 28672 | tf_op jit(solution)/shard_map/psum | solution.py:182
  (589 shorter events, 370.9 us)
Async XLA Ops:
  2.1 18.7 %collective-permute-start = (bf16[1024]{0:T(1024)(128)(2,1)S(1)}, bf16[1024]{0:T(1024)(128)(2,1)S(1)}, u32[]{:S(2)}, u32[]{:S(2)}) collective-permute-start(bf16[1024]{0:T(1024)(128)(2,1)S(1)} %and_select_fusion.2), channel_id=1, source_target_pairs={{0,128},{128,0},{4,132},{132,4},{8,136},{136,8},{12,140},{140,12},... | collective-permute-start | bytes 6152 | tf_op jit(solution)/shard_map/ppermute | solution.py:24
  6.6 97.8 %collective-permute-start.13 = (s32[3,1024]{1,0:T(4,128)S(1)}, s32[3,1024]{1,0:T(4,128)S(1)}, u32[]{:S(2)}, u32[]{:S(2)}) collective-permute-start(s32[3,1024]{1,0:T(4,128)S(1)} %concatenate.74), channel_id=1, source_target_pairs={{0,128},{128,0},{4,132},{132,4},{8,136},{136,8},{12,140},{140,12},... | collective-permute-start | bytes 36872 | tf_op jit(solution)/shard_map/ppermute | solution.py:24
  7.4 285.6 %collective-permute-start.1 = (s32[32,1024]{1,0:T(8,128)S(1)}, s32[32,1024]{1,0:T(8,128)S(1)}, u32[]{:S(2)}, u32[]{:S(2)}) collective-permute-start(s32[32,1024]{1,0:T(8,128)S(1)} %concatenate.78), channel_id=1, source_target_pairs={{0,128},{128,0},{4,132},{132,4},{8,136},{136,8},{12,140},{140,12},... | collective-permute-start | bytes 393224 | tf_op jit(solution)/shard_map/ppermute | solution.py:24
  12.1 306.9 %collective-permute-start.2 = (bf16[1024,128]{1,0:T(8,128)(2,1)}, bf16[1024,128]{1,0:T(8,128)(2,1)}, u32[]{:S(2)}, u32[]{:S(2)}) collective-permute-start(bf16[1024,128]{1,0:T(8,128)(2,1)} %concatenate.80), channel_id=1, source_target_pairs={{0,128},{128,0},{4,132},{132,4},{8,136},{136,8},{12,140},{140,12},... | collective-permute-start | bytes 786440 | tf_op jit(solution)/shard_map/ppermute | solution.py:24
  111.1 84.0 %collective-permute-start.25 = (s32[3,1024]{0,1:T(8,128)S(1)}, s32[3,1024]{0,1:T(8,128)S(1)}, u32[]{:S(2)}, u32[]{:S(2)}) collective-permute-start(s32[3,1024]{0,1:T(8,128)S(1)} %bitcast_select_fusion.2), channel_id=1, source_target_pairs={{0,64},{64,0},{4,68},{68,4},{8,72},{72,8},{12,76},{76,12},{16,80},... | collective-permute-start | bytes 36872 | tf_op jit(solution)/shard_map/ppermute | solution.py:24
  199.6 10.6 %collective-permute-start.26 = (bf16[1024]{0:T(1024)(128)(2,1)S(1)}, bf16[1024]{0:T(1024)(128)(2,1)S(1)}, u32[]{:S(2)}, u32[]{:S(2)}) collective-permute-start(bf16[1024]{0:T(1024)(128)(2,1)S(1)} %and_select_fusion), channel_id=1, source_target_pairs={{0,32},{32,0},{4,36},{36,4},{8,40},{40,8},{12,44},{44,12},{16,48},... | collective-permute-start | bytes 6152 | tf_op jit(solution)/shard_map/ppermute | solution.py:24
  298.8 10.4 %collective-permute-start.15 = (s32[32,1024]{0,1:T(8,128)S(1)}, s32[32,1024]{0,1:T(8,128)}, u32[]{:S(2)}, u32[]{:S(2)}) collective-permute-start(s32[32,1024]{0,1:T(8,128)S(1)} %bitcast_select_fusion.3), channel_id=1, source_target_pairs={{0,64},{64,0},{4,68},{68,4},{8,72},{72,8},{12,76},{76,12},{16,80},... | collective-permute-start | bytes 393224 | tf_op jit(solution)/shard_map/ppermute | solution.py:24
  315.7 20.2 %collective-permute-start.27 = (s32[32,1024]{0,1:T(8,128)S(1)}, s32[32,1024]{0,1:T(8,128)}, u32[]{:S(2)}, u32[]{:S(2)}) collective-permute-start(s32[32,1024]{0,1:T(8,128)S(1)} %bitcast_select_fusion.1), channel_id=1, source_target_pairs={{0,32},{32,0},{4,36},{36,4},{8,40},{40,8},{12,44},{44,12},{16,48},... | collective-permute-start | bytes 393224 | tf_op jit(solution)/shard_map/ppermute | solution.py:24
  364.8 6.5 collective-permute-start.9
  371.3 9.9 %collective-permute-start.10 = (f32[8,64]{1,0:T(8,128)S(1)}, f32[8,64]{1,0:T(8,128)S(1)}, u32[]{:S(2)}, u32[]{:S(2)}) collective-permute-start(f32[8,64]{1,0:T(8,128)S(1)} %slice_select_fusion.26), channel_id=1, source_target_pairs={{0,16},{16,0},{4,20},{20,4},{8,24},{24,8},{12,28},{28,12},{32,48},... | collective-permute-start | bytes 6152 | tf_op jit(solution)/shard_map/ppermute | solution.py:24
  379.9 10.8 %collective-permute-start.16 = (bf16[1024,128]{1,0:T(8,128)(2,1)S(1)}, bf16[1024,128]{1,0:T(8,128)(2,1)}, u32[]{:S(2)}, u32[]{:S(2)}) collective-permute-start(bf16[1024,128]{1,0:T(8,128)(2,1)S(1)} %get-tuple-element.1187), channel_id=1, source_target_pairs={{0,64},{64,0},{4,68},{68,4},{8,72},{72,8},{12,76},{76,12},{16,80},... | collective-permute-start | bytes 786440 | tf_op jit(solution)/shard_map/ppermute | solution.py:24
  381.2 9.5 %collective-permute-start.11 = (f32[4,64]{1,0:T(4,128)S(1)}, f32[4,64]{1,0:T(4,128)S(1)}, u32[]{:S(2)}, u32[]{:S(2)}) collective-permute-start(f32[4,64]{1,0:T(4,128)S(1)} %slice_select_fusion.28), channel_id=1, source_target_pairs={{0,8},{8,0},{4,12},{12,4},{16,24},{24,16},{20,28},{28,20},{32,40},... | collective-permute-start | bytes 3080 | tf_op jit(solution)/shard_map/ppermute | solution.py:24
  388.2 112.1 %collective-permute-start.3 = (f32[32,8192]{1,0:T(8,128)}, f32[32,8192]{1,0:T(8,128)}, u32[]{:S(2)}, u32[]{:S(2)}) collective-permute-start(f32[32,8192]{1,0:T(8,128)} %select_n.551), channel_id=1, source_target_pairs={{0,64},{64,0},{4,68},{68,4},{8,72},{72,8},{12,76},{76,12},{16,80},... | collective-permute-start | bytes 3145736 | tf_op jit(solution)/shard_map/ppermute | solution.py:24
  418.1 8.6 collective-permute-start.21
  420.2 7.2 collective-permute-start.12
  426.7 4.5 collective-permute-start.22
  427.7 16.2 %collective-permute-start.28 = (bf16[1024,128]{1,0:T(8,128)(2,1)S(1)}, bf16[1024,128]{1,0:T(8,128)(2,1)}, u32[]{:S(2)}, u32[]{:S(2)}) collective-permute-start(bf16[1024,128]{1,0:T(8,128)(2,1)S(1)} %get-tuple-element.1189), channel_id=1, source_target_pairs={{0,32},{32,0},{4,36},{36,4},{8,40},{40,8},{12,44},{44,12},{16,48},... | collective-permute-start | bytes 786440 | tf_op jit(solution)/shard_map/ppermute | solution.py:24
  431.2 12.7 %collective-permute-start.23 = (f32[8,64]{1,0:T(8,128)S(1)}, f32[8,64]{1,0:T(8,128)S(1)}, u32[]{:S(2)}, u32[]{:S(2)}) collective-permute-start(f32[8,64]{1,0:T(8,128)S(1)} %slice_select_fusion.25), channel_id=1, source_target_pairs={{0,8},{8,0},{4,12},{12,4},{16,24},{24,16},{20,28},{28,20},{32,40},... | collective-permute-start | bytes 6152 | tf_op jit(solution)/shard_map/ppermute | solution.py:24
  437.7 67.3 %collective-permute-start.17 = (f32[32,8192]{1,0:T(8,128)}, f32[32,8192]{1,0:T(8,128)}, u32[]{:S(2)}, u32[]{:S(2)}) collective-permute-start(f32[32,8192]{1,0:T(8,128)} %select_n.589), channel_id=1, source_target_pairs={{0,32},{32,0},{4,36},{36,4},{8,40},{40,8},{12,44},{44,12},{16,48},... | collective-permute-start | bytes 3145736 | tf_op jit(solution)/shard_map/ppermute | solution.py:24
  465.7 26.0 %collective-permute-start.32 = (f32[32,64]{1,0:T(8,128)S(1)}, f32[32,64]{1,0:T(8,128)S(1)}, u32[]{:S(2)}, u32[]{:S(2)}) collective-permute-start(f32[32,64]{1,0:T(8,128)S(1)} %select_n.632), channel_id=1, source_target_pairs={{0,16},{16,0},{4,20},{20,4},{8,24},{24,8},{12,28},{28,12},{32,48},... | collective-permute-start | bytes 24584 | tf_op jit(solution)/shard_map/ppermute | solution.py:24
  465.8 26.0 %collective-permute-start.24 = (f32[4,64]{1,0:T(4,128)S(1)}, f32[4,64]{1,0:T(4,128)S(1)}, u32[]{:S(2)}, u32[]{:S(2)}) collective-permute-start(f32[4,64]{1,0:T(4,128)S(1)} %slice_select_fusion.27), channel_id=1, source_target_pairs={{0,4},{4,0},{8,12},{12,8},{16,20},{20,16},{24,28},{28,24},{32,36},... | collective-permute-start | bytes 3080 | tf_op jit(solution)/shard_map/ppermute | solution.py:24
  494.3 5.8 collective-permute-start.34
  499.5 82.2 %collective-permute-start.29 = (f32[32,8192]{1,0:T(8,128)}, f32[32,8192]{1,0:T(8,128)}, u32[]{:S(2)}, u32[]{:S(2)}) collective-permute-start(f32[32,8192]{1,0:T(8,128)} %select_n.621), channel_id=1, source_target_pairs={{0,16},{16,0},{4,20},{20,4},{8,24},{24,8},{12,28},{28,12},{32,48},... | collective-permute-start | bytes 3145736 | tf_op jit(solution)/shard_map/ppermute | solution.py:24
  501.8 81.4 %collective-permute-start.4 = (f32[16,8192]{1,0:T(8,128)S(1)}, f32[16,8192]{1,0:T(8,128)S(1)}, u32[]{:S(2)}, u32[]{:S(2)}) collective-permute-start(f32[16,8192]{1,0:T(8,128)S(1)} %slice_select_fusion.9), channel_id=1, source_target_pairs={{0,32},{32,0},{4,36},{36,4},{8,40},{40,8},{12,44},{44,12},{16,48},... | collective-permute-start | bytes 1572872 | tf_op jit(solution)/shard_map/ppermute | solution.py:24
  506.4 86.4 %collective-permute-start.18 = (f32[16,8192]{1,0:T(8,128)S(1)}, f32[16,8192]{1,0:T(8,128)S(1)}, u32[]{:S(2)}, u32[]{:S(2)}) collective-permute-start(f32[16,8192]{1,0:T(8,128)S(1)} %slice_select_fusion.8), channel_id=1, source_target_pairs={{0,16},{16,0},{4,20},{20,4},{8,24},{24,8},{12,28},{28,12},{32,48},... | collective-permute-start | bytes 1572872 | tf_op jit(solution)/shard_map/ppermute | solution.py:24
  583.0 35.7 %collective-permute-start.30 = (f32[16,8192]{1,0:T(8,128)S(1)}, f32[16,8192]{1,0:T(8,128)S(1)}, u32[]{:S(2)}, u32[]{:S(2)}) collective-permute-start(f32[16,8192]{1,0:T(8,128)S(1)} %slice_select_fusion.7), channel_id=1, source_target_pairs={{0,8},{8,0},{4,12},{12,4},{16,24},{24,16},{20,28},{28,20},{32,40},... | collective-permute-start | bytes 1572872 | tf_op jit(solution)/shard_map/ppermute | solution.py:24
  583.3 20.8 %collective-permute-start.5 = (f32[8,8192]{1,0:T(8,128)S(1)}, f32[8,8192]{1,0:T(8,128)S(1)}, u32[]{:S(2)}, u32[]{:S(2)}) collective-permute-start(f32[8,8192]{1,0:T(8,128)S(1)} %slice_select_fusion.12), channel_id=1, source_target_pairs={{0,16},{16,0},{4,20},{20,4},{8,24},{24,8},{12,28},{28,12},{32,48},... | collective-permute-start | bytes 786440 | tf_op jit(solution)/shard_map/ppermute | solution.py:24
  604.2 8.2 collective-permute-start.6
  604.6 13.4 %collective-permute-start.19 = (f32[8,8192]{1,0:T(8,128)S(1)}, f32[8,8192]{1,0:T(8,128)S(1)}, u32[]{:S(2)}, u32[]{:S(2)}) collective-permute-start(f32[8,8192]{1,0:T(8,128)S(1)} %slice_select_fusion.11), channel_id=1, source_target_pairs={{0,8},{8,0},{4,12},{12,4},{16,24},{24,16},{20,28},{28,20},{32,40},... | collective-permute-start | bytes 786440 | tf_op jit(solution)/shard_map/ppermute | solution.py:24
  612.5 6.5 collective-permute-start.7
  618.1 4.3 collective-permute-start.20
  618.9 7.2 collective-permute-start.31
  (24 other events, 253.7 us)
